TPU v7x, 32 devices: a whole 2x2x4 slice. The times are simulated.
32 devices in a mesh: depth: 2 (over x), tile: 16 (over z, y, core).
Axes of the slice: x: 2, y: 2, z: 4, core: 2. Of those that a mesh axis runs over, the one named last changes fastest.
Arguments:
- exit_grad: bfloat16 [64, 256, 2, 256], P('tile', 'depth'), may hold values from -6 to 6
- stored_waves: bfloat16 [4, 64, 256, 2, 256], P('depth', 'tile'), may hold values from -6 to 6
- object_slices: float32 [4, 448, 2, 4096], P('depth', None, None, 'tile'), may hold values from -4 to 4
- propagator_taps: float32 [2, 2, 31], replicated, may hold values from -0.75 to 0.75
- positions: int32 [64, 2], replicated, may hold values from 0 to 255, as said below
- counts: int32 [16], replicated, may hold values from 1 to 4, as said below
Outputs:
- object_grad: bfloat16 [4, 448, 2, 4096], P('depth', None, None, 'tile')
Inputs may be any that keep to these rules, and one draw needn't show every extreme that they name: Column 0 is a window's first row, 0 to 192; column 1 is a window's centre column within its tile, 0 to 255. Dead slots hold positions too. `counts`: some tile has exactly 4 live slots and some tile exactly 1.
All inputs are finite; a program needn't handle non-finite values.
Results may differ from a plain program's by a relative error of at most 0.034.
Values may be sent and summed in bfloat16 or wider, within the bound.
No kernel may reach another device: no remote copies, remote signals or barrier semaphores. Data moves between devices by JAX's collectives and lax.ppermute only.
A program may use at most 64 MiB of HBM per device.

v0:
```python
import functools

import jax
import jax.numpy as jnp
from jax import lax
from jax.experimental import pallas as pl
from jax.experimental.pallas import tpu as pltpu
from jax.sharding import PartitionSpec as P


LANES = 128
CHUNK = 64
STEP = 32
PACKED = 16
F32 = jnp.float32
BF16 = jnp.bfloat16
VMEM = pl.BlockSpec(memory_space=pltpu.VMEM)
SMEM = pl.BlockSpec(memory_space=pltpu.SMEM)
HBM = pl.BlockSpec(memory_space=pltpu.HBM)


def as_rows(x):
    *lead, parts, columns = x.shape
    tiles = columns // LANES
    split = x.reshape(*lead, parts, tiles, LANES)
    return jnp.swapaxes(split, -3, -2).reshape(-1, LANES)


def from_rows(x, shape):
    *lead, parts, columns = shape
    tiles = columns // LANES
    split = x.reshape(*lead, tiles, parts, LANES)
    return jnp.swapaxes(split, -3, -2).reshape(shape)


def row_ids(start, rows):
    return lax.broadcasted_iota(jnp.int32, (rows, LANES), 0) + start


def lane_ids(rows):
    return lax.broadcasted_iota(jnp.int32, (rows, LANES), 1)


class Place:
    def __init__(self, info, j, cap):
        self.row = info[3 + j]
        self.col = info[3 + cap + j]
        self.mixed = jnp.where(self.col < LANES, 0, 1)

    def halo_first(self, total_rows, halo_rows):
        return pl.multiple_of(jnp.minimum(self.row // PACKED * PACKED, total_rows - halo_rows), PACKED)

    def on_halo(self, rows):
        column = lane_ids(rows) + self.mixed * LANES
        return (column >= self.col) == (self.mixed == 0)


def first_kernel(
    counts,
    positions,
    taps,
    obj_in,
    cross_edge,
    chip_edge,
    info,
    taps_out,
    obj,
    counts_in,
    spots,
    small_sem,
    obj_sem,
):
    cap = (info.shape[0] - 3) // 2
    slices, parts, rows, _ = cross_edge.shape
    pieces = obj_sem.shape[0]
    piece_rows = slices * rows // pieces

    def copy(source, target, sem):
        return pltpu.make_async_copy(source, target, sem)

    small = [
        copy(source, target, small_sem.at[i])
        for i, (source, target) in enumerate(((counts, counts_in), (positions, spots), (taps, taps_out)))
    ]
    loads = []
    for p in range(pieces):
        part = pl.ds(p * piece_rows * 4, piece_rows * 4)
        loads.append(copy(obj_in.at[part], obj.at[part], obj_sem.at[p]))
    for each in loads + small:
        each.start()
    tile = lax.axis_index("tile")
    cross_side = tile % 2
    for p in range(pieces):
        loads[p].wait()
        s, first = divmod(p * piece_rows, rows)
        start = p * piece_rows * 4
        for c in range(parts):
            beyond = obj[pl.ds(start + cross_side * 2 + c, piece_rows, stride=4), :]
            beside = obj[pl.ds(start + (1 - cross_side) * 2 + c, piece_rows, stride=4), :]
            cross_edge[s, c, pl.ds(first, piece_rows), :] = beyond.astype(BF16)
            chip_edge[s, c, pl.ds(first, piece_rows), :] = beside.astype(BF16)
    for each in small:
        each.wait()
    info[0] = lax.axis_index("depth")
    info[1] = tile
    info[2] = counts_in[tile]
    for j in range(cap):
        info[3 + j] = spots[0, tile * cap + j]
        info[3 + cap + j] = spots[1, tile * cap + j]


def build_blocks(taps, blocks):
    tap_count = taps.shape[2]
    centre = tap_count // 2

    def tap(m, k):
        return taps[1, m, k] if m < 2 else taps[0, m - 2, tap_count - 1 - k]

    def build(block, first, shift, ks):
        diff = lane_ids(STEP) - row_ids(first, STEP) + shift
        total = [jnp.zeros((STEP, LANES), F32) for _ in range(4)]
        for k in ks:
            hit = diff == k - centre
            for m in range(4):
                total[m] = jnp.where(hit, tap(m, k), total[m])
        for m in range(4):
            blocks[m, block, pl.ds(first, STEP), :] = total[m]

    def diagonal(i, carry):
        build(0, pl.multiple_of(i * STEP, STEP), 0, range(tap_count))
        return carry

    lax.fori_loop(0, LANES // STEP, diagonal, 0)
    for first in range(0, LANES, STEP):
        build(1, first, LANES, range(centre + 1, tap_count) if first + STEP == LANES else ())
        build(2, first, -LANES, range(centre) if first == 0 else ())


def matrices_kernel(info, taps, col_mat, row_mat, blocks):
    cap = col_mat.shape[0]
    side = row_mat.shape[0]
    build_blocks(taps, blocks)

    def rows_of(i, tile_row):
        return pl.ds(pl.multiple_of(i * STEP + tile_row * LANES, STEP), STEP)

    def low_rows_of(i, tile_row):
        return pl.ds(pl.multiple_of(i * STEP + tile_row * LANES + side, STEP), STEP)

    def row_part(i, carry):
        for tr in range(2):
            for tc in range(2):
                block = 0 if tr == tc else 1 + tr
                for c in range(2):
                    value = blocks[2 + c, block, pl.ds(pl.multiple_of(i * STEP, STEP), STEP), :]
                    row_mat[rows_of(i, tr), pl.ds(tc * LANES + c * side, LANES)] = value.astype(BF16)
        return carry

    lax.fori_loop(0, LANES // STEP, row_part, 0)

    def slot(j, carry):
        seam = Place(info, j, cap).col

        def fill(i, inner):
            first = pl.multiple_of(i * STEP, STEP)
            for tr in range(2):
                for tc in range(2):
                    row_side = row_ids(first, STEP) + tr * LANES >= seam
                    col_side = lane_ids(STEP) + tc * LANES >= seam
                    same = row_side == col_side
                    values = []
                    for m in range(2):
                        if tr == tc:
                            close, far = blocks[m, 0, pl.ds(first, STEP), :], 0.0
                        else:
                            close = blocks[m, 1 + tr, pl.ds(first, STEP), :]
                            far = blocks[m, 2 - tr, pl.ds(first, STEP), :]
                        values.append(jnp.where(same, close, far))
                    re, im = values[0].astype(BF16), values[1].astype(BF16)
                    re_cols = pl.ds(tc * LANES, LANES)
                    im_cols = pl.ds(tc * LANES + side, LANES)
                    col_mat[j, rows_of(i, tr), re_cols] = re
                    col_mat[j, rows_of(i, tr), im_cols] = -im
                    col_mat[j, low_rows_of(i, tr), re_cols] = im
                    col_mat[j, low_rows_of(i, tr), im_cols] = re
            return inner

        return lax.fori_loop(0, LANES // STEP, fill, carry)

    lax.fori_loop(0, info[2], slot, 0)


def take_halo(info, place, across, inside, halo):
    rows = pl.ds(place.halo_first(across.shape[2], halo.shape[2]), halo.shape[2])
    from_across = place.mixed == info[1] % 2

    @pl.when(from_across)
    def _():
        halo[...] = across[:, :, rows, :].astype(F32)

    @pl.when(jnp.logical_not(from_across))
    def _():
        halo[...] = inside[:, :, rows, :].astype(F32)


def unpack(place, sources, wide, write):
    side = 0
    for packed, start, count in sources:
        wide[pl.ds(side * 4, count * 4), :] = packed[pl.ds(start, count * 4), :].astype(F32)
        side += count

    def move(i, carry):
        a = pl.multiple_of(i * CHUNK, CHUNK)
        for c in range(2):
            halves = [wide[pl.ds(a * 4 + ct * 2 + c, CHUNK, stride=4), :] for ct in range(2)]
            value = pltpu.roll(jnp.concatenate(halves, axis=1), place.col, 1)
            write(c, pl.ds(a, CHUNK), value.astype(BF16))
        return carry

    lax.fori_loop(0, side // CHUNK, move, 0)


def unpack_stored(place, j, cap, stored, planes, packed, sems, wide):
    slices, _, side, _ = planes.shape

    def load(s):
        start = pl.multiple_of((s * cap + j) * side * 4, side * 4)
        return pltpu.make_async_copy(stored.at[pl.ds(start, side * 4)], packed.at[s], sems.at[s])

    def begin(s, carry):
        load(s).start()
        return carry

    def one(s, carry):
        def write(c, rows, value):
            planes[s, c, rows] = value

        load(s).wait()
        unpack(place, [(packed.at[s], 0, side)], wide, write)
        return carry

    lax.fori_loop(0, slices, begin, 0)
    lax.fori_loop(0, slices, one, 0)


def back(j, wave, col_mat, row_mat, rhs, h_buf, s):
    side = wave.shape[0]
    mixed = jnp.dot(wave[...], col_mat[j], preferred_element_type=F32).astype(BF16)
    rhs[:side, :] = mixed
    rhs[side:, :side] = mixed[:, side:]
    rhs[side:, side:] = -mixed[:, :side]
    h_buf[s] = jnp.dot(row_mat[...], rhs[...], preferred_element_type=F32)


def tile_columns(ct, c, side):
    return pl.ds(pl.multiple_of(ct * LANES + c * side, LANES), LANES)


def leave(place, s, a, obj, halo, h_buf, wave):
    side = wave.shape[0]
    total_rows = obj.shape[0] // h_buf.shape[0] // 4
    halo_row = place.row - place.halo_first(total_rows, halo.shape[2]) + a
    rows = pl.ds(a, CHUNK)
    on_halo = place.on_halo(CHUNK)
    for ct, own in ((place.mixed, 1 - place.mixed), (1 - place.mixed, place.mixed)):
        o = []
        for c in range(2):
            first = (s * total_rows + place.row + a) * 4 + own * 2 + c
            value = obj[pl.ds(first, CHUNK, stride=4), :]
            if ct is place.mixed:
                beyond = halo[s, c, pl.ds(halo_row, CHUNK), :]
                value = jnp.where(on_halo, beyond, value)
            o.append(value)
        h_re = h_buf[s, rows, tile_columns(ct, 0, side)]
        h_im = h_buf[s, rows, tile_columns(ct, 1, side)]
        wave[rows, tile_columns(ct, 0, side)] = (o[0] * h_re + o[1] * h_im).astype(BF16)
        wave[rows, tile_columns(ct, 1, side)] = (o[0] * h_im - o[1] * h_re).astype(BF16)


def collect(place, s, a, planes, h_buf, own_sums, halo_sums):
    side = h_buf.shape[1]
    rows = pl.ds(a, CHUNK)
    frame_rows = pl.ds(place.row + a, CHUNK)
    on_halo = place.on_halo(CHUNK)
    for ct, own in ((place.mixed, 1 - place.mixed), (1 - place.mixed, place.mixed)):
        cols = tile_columns(ct, 0, side)
        st_re = planes[s, 0, rows, cols].astype(F32)
        st_im = planes[s, 1, rows, cols].astype(F32)
        h_re = h_buf[s, rows, cols]
        h_im = h_buf[s, rows, tile_columns(ct, 1, side)]
        for c, g in enumerate((st_re * h_re + st_im * h_im, st_re * h_im - st_im * h_re)):
            if ct is place.mixed:
                halo_sums[place.mixed, s, c, frame_rows, :] += jnp.where(on_halo, g, 0.0)
                own_sums[own, s, c, frame_rows, :] += jnp.where(on_halo, 0.0, g)
            else:
                own_sums[own, s, c, frame_rows, :] += g


def each_chunk(side, body):
    def step(k, carry):
        body(pl.multiple_of(k * CHUNK, CHUNK))
        return carry

    lax.fori_loop(0, side // CHUNK, step, 0)


def each_slice(slices, body):
    def step(i, carry):
        body(slices - 1 - i)
        return carry

    lax.fori_loop(0, slices, step, 0)


def take_exit(place, j, incoming, out, wide):
    side = out.shape[0]
    count = side // len(incoming)

    def write(c, rows, value):
        out[rows, pl.ds(c * side, side)] = value

    unpack(place, [(ref, j * count * 4, count) for ref in incoming], wide, write)


def start_kernel(groups, n_in, *refs):
    info, col_mat, row_mat = refs[:3]
    incoming = refs[3 : 3 + n_in]
    h_buf, out, wide, rhs = refs[3 + n_in :]
    place = Place(info, 0, col_mat.shape[0])

    @pl.when(info[0] == groups - 1)
    def _():
        take_exit(place, 0, incoming, out, wide)
        back(0, out, col_mat, row_mat, rhs, h_buf, 0)


def resume_kernel(
    groups,
    info,
    stored,
    obj,
    across,
    inside,
    col_mat,
    row_mat,
    old_h,
    out,
    h_buf,
    planes,
    halo,
    rhs,
    wide,
    packed,
    sems,
):
    slices, side = h_buf.shape[:2]
    place = Place(info, 0, col_mat.shape[0])
    take_halo(info, place, across, inside, halo)

    @pl.when(info[0] == groups - 1)
    def _():
        h_buf[slices - 1] = old_h[0]

        def one_slice(s):
            each_chunk(side, lambda a: leave(place, s, a, obj, halo, h_buf, out))

            @pl.when(s > 0)
            def _():
                back(0, out, col_mat, row_mat, rhs, h_buf, s - 1)

        each_slice(slices, one_slice)

    @pl.when(info[0] != groups - 1)
    def _():
        unpack_stored(place, 0, col_mat.shape[0], stored, planes, packed, sems, wide)


def forward_kernel(groups, j, group, n_in, *refs):
    info, stored, obj, across, inside, col_mat, row_mat = refs[:7]
    incoming = refs[7 : 7 + n_in]
    out, h_buf, planes, halo, wide, rhs, packed, sems = refs[7 + n_in :]
    slices, side = h_buf.shape[:2]
    cap = col_mat.shape[0]
    last = group == groups - 1
    place = Place(info, j, cap)
    take_halo(info, place, across, inside, halo)

    @pl.when(info[0] == group)
    def _():
        if last:
            take_exit(place, j, incoming, out, wide)
        else:
            out[...] = incoming[0][...]

        def one_slice(s):
            back(j, out, col_mat, row_mat, rhs, h_buf, s)
            each_chunk(side, lambda a: leave(place, s, a, obj, halo, h_buf, out))

        each_slice(slices, one_slice)

    if last:

        @pl.when(info[0] != group)
        def _():
            unpack_stored(place, j, cap, stored, planes, packed, sems, wide)


def grad_kernel(groups, j, *refs):
    info, stored, obj, col_mat, row_mat, halo, planes_in, received, h_last = refs[:9]
    own_sums, halo_sums, wave, rhs, h_buf, planes, wide, packed, sems = refs[-9:]
    slices, side = h_last.shape[:2]
    cap = col_mat.shape[0]
    place = Place(info, j, cap)
    if j == 0:
        own_sums[...] = jnp.zeros(own_sums.shape, F32)
        halo_sums[...] = jnp.zeros(halo_sums.shape, F32)

    @pl.when(info[0] == groups - 1)
    def _():
        unpack_stored(place, j, cap, stored, planes, packed, sems, wide)
        each_slice(
            slices,
            lambda s: each_chunk(side, lambda a: collect(place, s, a, planes, h_last, own_sums, halo_sums)),
        )

    @pl.when(info[0] != groups - 1)
    def _():
        wave[...] = received[...]

        def one_slice(s):
            back(j, wave, col_mat, row_mat, rhs, h_buf, s)

            @pl.when(s > 0)
            def _():
                each_chunk(side, lambda a: leave(place, s, a, obj, halo, h_buf, wave))

            each_chunk(side, lambda a: collect(place, s, a, planes_in, h_buf, own_sums, halo_sums))

        each_slice(slices, one_slice)


def rims_kernel(info, own_sums, halo_sums, cross_rim, chip_rim, own):
    side = info[1] % 2
    cross_rim[...] = halo_sums[side].astype(BF16)
    chip_rim[...] = halo_sums[1 - side].astype(BF16)
    own[...] = own_sums[...].astype(BF16)


def add_rim(own, ct, rim, mix, s):
    _, _, parts, rows, _ = own.shape
    for c in range(parts):
        total = own[ct, s, c].astype(F32) + rim[s, c].astype(F32)
        mix[pl.ds(s * rows * 4 + ct * 2 + c, rows, stride=4), :] = total


def inside_kernel(info, own, rim, mix):
    for s in range(own.shape[1]):
        add_rim(own, 1 - info[1] % 2, rim, mix, s)


def close_kernel(info, own, rim, mix_in, out, mix, packed, sems):
    slices = own.shape[1]
    length = mix.shape[0] // slices
    copies = []
    for s in range(slices):
        part = pl.ds(s * length, length)
        add_rim(own, info[1] % 2, rim, mix, s)
        packed[part, :] = mix[part, :].astype(BF16)
        copies.append(pltpu.make_async_copy(packed.at[part], out.at[part], sems.at[s]))
        copies[-1].start()
    for copy in copies:
        copy.wait()


def near(x):
    return pltpu.with_memory_space_constraint(x, pltpu.VMEM)


def far(x):
    return pltpu.with_memory_space_constraint(x, pltpu.HBM)


def kernel_call(body, scalars, arrays, out, scratch=(), aliases=None, mib=8, distant=()):
    single = not isinstance(out, tuple)
    specs = tuple(SMEM if o.memory_space == pltpu.SMEM else VMEM for o in ((out,) if single else out))
    return pl.pallas_call(
        body,
        out_shape=out,
        in_specs=[SMEM] * len(scalars) + [HBM] * len(distant) + [VMEM] * len(arrays),
        out_specs=specs[0] if single else specs,
        scratch_shapes=list(scratch),
        input_output_aliases=aliases or {},
        compiler_params=pltpu.CompilerParams(vmem_limit_bytes=mib << 20),
    )(*scalars, *[far(a) for a in distant], *[near(a) for a in arrays])


def on_device(exit_grad, stored_waves, object_slices, propagator_taps, positions, counts):
    slices, cap, side = stored_waves.shape[:3]
    rows = object_slices.shape[1]
    groups = lax.axis_size("depth")
    tiles = lax.axis_size("tile")
    group_index = lax.axis_index("depth")
    across = [(i, (i + 1) % tiles if i % 2 else (i - 1) % tiles) for i in range(tiles)]
    inside = [(i, i ^ 1) for i in range(tiles)]

    def moved(x, pairs):
        return lax.ppermute(x, "tile", pairs)

    def swap(x, one, other):
        return lax.ppermute(x, "depth", [(one, other), (other, one)])

    moved_exits = [swap(exit_grad, g, groups - 1) for g in range(groups - 1)]
    exits = [as_rows(x) for x in moved_exits + [exit_grad]]

    obj_shape = pltpu.VMEM((slices * rows * 4, LANES), F32)
    wave_shape = pltpu.VMEM((side, 2 * side), BF16)
    wide_scratch = pltpu.VMEM((side * 4, LANES), F32)
    edge_shapes = (pltpu.VMEM((slices, 2, rows, LANES), BF16),) * 2
    spots = positions.T
    pieces = slices * 2 if rows % (2 * PACKED) == 0 else slices
    cross_edge, chip_edge, info, taps, obj = pl.pallas_call(
        first_kernel,
        out_shape=(
            *edge_shapes,
            pltpu.SMEM((3 + 2 * cap,), jnp.int32),
            pltpu.SMEM(propagator_taps.shape, F32),
            obj_shape,
        ),
        in_specs=[HBM] * 4,
        out_specs=(VMEM, VMEM, SMEM, SMEM, VMEM),
        scratch_shapes=[
            pltpu.SMEM(counts.shape, jnp.int32),
            pltpu.SMEM(spots.shape, jnp.int32),
            pltpu.SemaphoreType.DMA((3,)),
            pltpu.SemaphoreType.DMA((pieces,)),
        ],
        compiler_params=pltpu.CompilerParams(vmem_limit_bytes=8 << 20),
        name="first",
    )(*[far(a) for a in (counts, spots, propagator_taps, as_rows(object_slices))])
    from_across = moved(cross_edge, across)
    from_inside = moved(chip_edge, inside)

    col_mats, row_mat = kernel_call(
        matrices_kernel,
        (info, taps),
        (),
        (pltpu.VMEM((cap, 2 * side, 2 * side), BF16), wave_shape),
        (pltpu.VMEM((4, 3, LANES, LANES), F32),),
    )
    mats = (col_mats, row_mat)
    stored = as_rows(stored_waves)
    rhs_scratch = pltpu.VMEM((2 * side, 2 * side), BF16)
    h_shape = pltpu.VMEM((slices, side, 2 * side), F32)
    halo_shape = pltpu.VMEM((slices, 2, side + PACKED, LANES), F32)
    planes_shape = pltpu.VMEM((slices, 2, side, side), BF16)
    sums_shape = pltpu.VMEM((2, slices, 2, rows, LANES), F32)

    packed_scratch = (
        pltpu.VMEM((slices, side * 4, LANES), BF16),
        pltpu.SemaphoreType.DMA((slices,)),
    )
    h_start = kernel_call(
        functools.partial(start_kernel, groups, len(exits)),
        (info,),
        (*mats, *exits),
        pltpu.VMEM((1, side, 2 * side), F32),
        (wave_shape, wide_scratch, rhs_scratch),
    )

    def resume():
        return kernel_call(
            functools.partial(resume_kernel, groups),
            (info,),
            (obj, from_across, from_inside, *mats, h_start),
            (wave_shape, h_shape, planes_shape, halo_shape),
            (rhs_scratch, wide_scratch, *packed_scratch),
            distant=(stored,),
        )

    def forward(j, group, incoming):
        return kernel_call(
            functools.partial(forward_kernel, groups, j, group, len(incoming)),
            (info,),
            (obj, from_across, from_inside, *mats, *incoming),
            (wave_shape, h_shape, planes_shape, halo_shape),
            (wide_scratch, rhs_scratch, *packed_scratch),
            distant=(stored,),
        )

    def gradient(j, received, h_last, planes, halo, sums):
        return kernel_call(
            functools.partial(grad_kernel, groups, j),
            (info,),
            (obj, *mats, halo, planes, received, h_last, *sums),
            (sums_shape, sums_shape),
            (wave_shape, rhs_scratch, h_shape, planes_shape, wide_scratch, *packed_scratch),
            {9: 0, 10: 1} if sums else {},
            distant=(stored,),
        )

    def with_live(live):
        def run():
            ready = [resume()]
            waves = [None] * live
            received = [None] * live
            for group in range(groups - 1, 0, -1):
                for j in range(live):
                    last = group == groups - 1
                    if not last:
                        sent = forward(j, group, [waves[j]])[0]
                    else:
                        if j > 0:
                            ready.append(forward(j, group, exits))
                        sent = ready[j][0]
                    arrived = swap(sent, group, group - 1)
                    waves[j] = arrived
                    mine = group_index == group - 1
                    received[j] = arrived if last else jnp.where(mine, arrived, received[j])
            sums = ()
            for j in range(live):
                sums = gradient(j, received[j], *ready[j][1:], sums)
            own_shape = pltpu.VMEM((2, slices, 2, rows, LANES), BF16)
            return kernel_call(rims_kernel, (info,), sums, (*edge_shapes, own_shape))

        return run

    cross_rim, chip_rim, own = lax.switch(info[2] - 1, [with_live(n + 1) for n in range(cap)])
    rim_across = moved(cross_rim, across)
    rim_inside = moved(chip_rim, inside)
    mix_shape = pltpu.VMEM((slices * rows * 4, LANES), F32)
    mix = kernel_call(inside_kernel, (info,), (own, rim_inside), mix_shape)
    out_rows, _ = pl.pallas_call(
        close_kernel,
        out_shape=(jax.ShapeDtypeStruct((slices * rows * 4, LANES), BF16), mix_shape),
        in_specs=[SMEM, VMEM, VMEM, VMEM],
        out_specs=(HBM, VMEM),
        scratch_shapes=[
            pltpu.VMEM((slices * rows * 4, LANES), BF16),
            pltpu.SemaphoreType.DMA((slices,)),
        ],
        input_output_aliases={3: 1},
        compiler_params=pltpu.CompilerParams(vmem_limit_bytes=8 << 20),
        name="close",
    )(info, near(own), near(rim_across), near(mix))
    return from_rows(out_rows, (slices, rows, 2, 2 * LANES))


def solution(mesh):
    return jax.shard_map(
        on_device,
        mesh=mesh,
        in_specs=(
            P("tile", "depth", None, None),
            P("depth", "tile", None, None, None),
            P("depth", None, None, "tile"),
            P(),
            P(),
            P(),
        ),
        out_specs=P("depth", None, None, "tile"),
        check_vma=False,
    )
```

profile of v0, /device:TPU:19, one launch (start us, length us, event | category | flops | bytes accessed | tf_op | source)
XLA Modules:
  0.0 59.1 jit_solution(5979792016435000887)
XLA Ops:
  0.0 0.0 copy-start
  0.0 0.3 collective-permute-start.12
  0.3 1.6 %first.1 = (bf16[2,2,448,128]{3,2,1,0:T(8,128)(2,1)S(1)}, bf16[2,2,448,128]{3,2,1,0:T(8,128)(2,1)S(1)}, s32[11]{0:T(128)S(4)}, f32[2,2,31]{2,1,0:T(2,128)S(4)}, f32[3584,128]{1,0:T(8,128)S(1)}) custom-call(s32[16]{0:T(128)} %counts.1, s32[2,64]{1,0:T(2,128)} %bitcast.40, f32[2,2,31]{2,1,0:T(2,128)} %taps.1, f32[3584,128]{1,0:T(8,128)} %bitcast.39), custom_call_target="tpu_custom_call" | custom-call | tf_op jit(solution)/shard_map/first/pallas_call | solution.py:521
  1.8 2.1 %collective-permute-start.10 = (bf16[2,2,448,128]{3,2,1,0:T(8,128)(2,1)S(1)}, bf16[2,2,448,128]{3,2,1,0:T(8,128)(2,1)S(1)}, u32[]{:S(2)}, u32[]{:S(2)}) collective-permute-start(bf16[2,2,448,128]{3,2,1,0:T(8,128)(2,1)S(1)} %get-tuple-element.192), channel_id=1, source_target_pairs={{0,15},{1,2},{2,1},{3,4},{4,3},{5,6},{6,5},{7,8},{8,7},{9,10},{10,... | collective-permute-start | bytes 1376264 | tf_op jit(solution)/shard_map/ppermute | solution.py:507
  4.0 0.0 collective-permute-start.11
  4.0 0.6 %slice.3 = s32[1]{0:T(128)} slice(s32[11]{0:T(128)S(4)} %get-tuple-element.190.info.refs_0_), slice={[2:3]} | slice | bytes 8 | tf_op jit(solution)/shard_map/slice | solution.py:627
  4.6 1.4 %shard_map.64 = (bf16[4,512,512]{2,1,0:T(8,128)(2,1)S(1)}, bf16[256,512]{1,0:T(8,128)(2,1)S(1)}) custom-call(s32[11]{0:T(128)S(4)} %get-tuple-element.190.info.refs_0_, f32[2,2,31]{2,1,0:T(2,128)S(4)} %get-tuple-element.194.taps), custom_call_target="tpu_custom_call" | custom-call | tf_op jit(solution)/shard_map/pallas_call | solution.py:486
  6.6 6.4 %collective-permute-done.12 = bf16[4,128,2,256]{3,2,1,0:T(2,128)(2,1)S(1)} collective-permute-done((bf16[4,128,2,256]{3,2,1,0:T(2,128)(2,1)}, bf16[4,128,2,256]{3,2,1,0:T(2,128)(2,1)S(1)}, u32[]{:S(2)}, u32[]{:S(2)}) %collective-permute-start.12) | collective-permute-done | bytes 524320 | tf_op jit(solution)/shard_map/ppermute | solution.py:510
  13.0 0.0 copy-done
  13.0 1.0 %shard_map.65 = f32[1,256,512]{2,1,0:T(8,128)S(1)} custom-call(s32[11]{0:T(128)S(4)} %get-tuple-element.190.info.refs_0_, bf16[4,512,512]{2,1,0:T(8,128)(2,1)S(1)} %get-tuple-element.195.refs_1_, bf16[256,512]{1,0:T(8,128)(2,1)S(1)} %get-tuple-element.196.refs_2_, bf16[2048,128]{1,0:T(8,128)(2,1)S(1)} %bitcast.31, bf16[2048,128]{1,0:T(8,128)(2,1)S(1)} %bitcast.27), custom_call_target="tpu_custom_call" | custom-call | tf_op jit(solution)/shard_map/pallas_call | solution.py:486
  14.0 1.1 %collective-permute-done.10 = bf16[2,2,448,128]{3,2,1,0:T(8,128)(2,1)S(1)} collective-permute-done((bf16[2,2,448,128]{3,2,1,0:T(8,128)(2,1)S(1)}, bf16[2,2,448,128]{3,2,1,0:T(8,128)(2,1)S(1)}, u32[]{:S(2)}, u32[]{:S(2)}) %collective-permute-start.10) | collective-permute-done | bytes 458784 | tf_op jit(solution)/shard_map/ppermute | solution.py:507
  15.1 0.0 collective-permute-done.11
  15.1 29.0 %conditional.1 = ((bf16[2,2,448,128]{3,2,1,0:T(8,128)(2,1)S(1)}, bf16[2,2,448,128]{3,2,1,0:T(8,128)(2,1)S(1)}, bf16[2,2,2,448,128]{4,3,2,1,0:T(8,128)(2,1)S(1)})) conditional(s32[]{:T(128)} %bitcast.4, (s32[11]{0:T(128)S(4)}, bf16[8192,128]{1,0:T(8,128)(2,1)}, f32[3584,128]{1,0:T(8,128)S(1)}, ...), branch_computations={%region_0.0_spmd, %region_1.0_spmd, %region_2.0_spmd, %region_3.0_... | conditional | bytes 4194472 | solution.py:627
  15.1 1.0 %branch_3_fun.12 = (bf16[256,512]{1,0:T(8,128)(2,1)S(1)}, f32[2,256,512]{2,1,0:T(8,128)S(1)}, bf16[2,2,256,256]{3,2,1,0:T(8,128)(2,1)S(1)}, f32[2,2,272,128]{3,2,1,0:T(8,128)S(1)}) custom-call(s32[11]{0:T(128)S(4)} %get-tuple-element.145.refs_0_.info, bf16[8192,128]{1,0:T(8,128)(2,1)} %get-tuple-element.146.refs_1_.stored, ...), custom_call_target="tpu_custom_call" | custom-call | tf_op jit(solution)/shard_map/cond/branch_3_fun/pallas_call | solution.py:486
  16.1 2.1 %collective-permute-start.9 = (bf16[256,512]{1,0:T(8,128)(2,1)S(1)}, bf16[256,512]{1,0:T(8,128)(2,1)S(1)}, u32[]{:S(2)}, u32[]{:S(2)}) collective-permute-start(bf16[256,512]{1,0:T(8,128)(2,1)S(1)} %get-tuple-element.169), channel_id=1, source_target_pairs={{16,0},{0,16},{17,1},{1,17},{18,2},{2,18},{19,3},{3,19},{20,4},{4,... | collective-permute-start | bytes 786440 | tf_op jit(solution)/shard_map/cond/branch_3_fun/ppermute | solution.py:510
  18.2 2.0 %branch_3_fun.11 = (bf16[256,512]{1,0:T(8,128)(2,1)S(1)}, f32[2,256,512]{2,1,0:T(8,128)S(1)}, bf16[2,2,256,256]{3,2,1,0:T(8,128)(2,1)S(1)}, f32[2,2,272,128]{3,2,1,0:T(8,128)S(1)}) custom-call(s32[11]{0:T(128)S(4)} %get-tuple-element.145.refs_0_.info, bf16[8192,128]{1,0:T(8,128)(2,1)} %get-tuple-element.146.refs_1_.stored, ...), custom_call_target="tpu_custom_call" | custom-call | tf_op jit(solution)/shard_map/cond/branch_3_fun/pallas_call | solution.py:486
  20.2 0.1 collective-permute-start.8
  20.3 2.0 %branch_3_fun.10 = (bf16[256,512]{1,0:T(8,128)(2,1)S(1)}, f32[2,256,512]{2,1,0:T(8,128)S(1)}, bf16[2,2,256,256]{3,2,1,0:T(8,128)(2,1)S(1)}, f32[2,2,272,128]{3,2,1,0:T(8,128)S(1)}) custom-call(s32[11]{0:T(128)S(4)} %get-tuple-element.145.refs_0_.info, bf16[8192,128]{1,0:T(8,128)(2,1)} %get-tuple-element.146.refs_1_.stored, ...), custom_call_target="tpu_custom_call" | custom-call | tf_op jit(solution)/shard_map/cond/branch_3_fun/pallas_call | solution.py:486
  22.3 1.4 %collective-permute-start.7 = (bf16[256,512]{1,0:T(8,128)(2,1)S(1)}, bf16[256,512]{1,0:T(8,128)(2,1)S(1)}, u32[]{:S(2)}, u32[]{:S(2)}) collective-permute-start(bf16[256,512]{1,0:T(8,128)(2,1)S(1)} %get-tuple-element.160), channel_id=1, source_target_pairs={{16,0},{0,16},{17,1},{1,17},{18,2},{2,18},{19,3},{3,19},{20,4},{4,... | collective-permute-start | bytes 786440 | tf_op jit(solution)/shard_map/cond/branch_3_fun/ppermute | solution.py:510
  23.6 2.2 %branch_3_fun.9 = (bf16[256,512]{1,0:T(8,128)(2,1)S(1)}, f32[2,256,512]{2,1,0:T(8,128)S(1)}, bf16[2,2,256,256]{3,2,1,0:T(8,128)(2,1)S(1)}, f32[2,2,272,128]{3,2,1,0:T(8,128)S(1)}) custom-call(s32[11]{0:T(128)S(4)} %get-tuple-element.145.refs_0_.info, bf16[8192,128]{1,0:T(8,128)(2,1)} %get-tuple-element.146.refs_1_.stored, ...), custom_call_target="tpu_custom_call" | custom-call | tf_op jit(solution)/shard_map/cond/branch_3_fun/pallas_call | solution.py:486
  25.8 0.1 collective-permute-start.6
  25.9 0.0 collective-permute-done.9.refs_7_
  25.9 2.4 %branch_3_fun.13 = (f32[2,2,2,448,128]{4,3,2,1,0:T(8,128)S(1)}, f32[2,2,2,448,128]{4,3,2,1,0:T(8,128)S(1)}) custom-call(s32[11]{0:T(128)S(4)} %get-tuple-element.145.refs_0_.info, bf16[8192,128]{1,0:T(8,128)(2,1)} %get-tuple-element.146.refs_1_.stored, f32[3584,128]{1,0:T(8,128)S(1)} %get-tuple-element.147.refs_2_.obj, ...), custom_call_target="tpu_custom_call" | custom-call | tf_op jit(solution)/shard_map/cond/branch_3_fun/pallas_call | solution.py:486
  28.3 1.9 %collective-permute-done.8.refs_7_ = bf16[256,512]{1,0:T(8,128)(2,1)S(1)} collective-permute-done((bf16[256,512]{1,0:T(8,128)(2,1)S(1)}, bf16[256,512]{1,0:T(8,128)(2,1)S(1)}, u32[]{:S(2)}, u32[]{:S(2)}) %collective-permute-start.8) | collective-permute-done | bytes 262176 | tf_op jit(solution)/shard_map/cond/branch_3_fun/ppermute | solution.py:510
  30.2 2.2 %branch_3_fun.14 = (f32[2,2,2,448,128]{4,3,2,1,0:T(8,128)S(1)}, f32[2,2,2,448,128]{4,3,2,1,0:T(8,128)S(1)}) custom-call(s32[11]{0:T(128)S(4)} %get-tuple-element.145.refs_0_.info, bf16[8192,128]{1,0:T(8,128)(2,1)} %get-tuple-element.146.refs_1_.stored, ...), custom_call_target="tpu_custom_call", output_to_operand_aliasing={{0}: (9, {}), {1}: (10, {})} | custom-call | tf_op jit(solution)/shard_map/cond/branch_3_fun/pallas_call | solution.py:486
  32.4 3.5 %collective-permute-done.7.refs_7_ = bf16[256,512]{1,0:T(8,128)(2,1)S(1)} collective-permute-done((bf16[256,512]{1,0:T(8,128)(2,1)S(1)}, bf16[256,512]{1,0:T(8,128)(2,1)S(1)}, u32[]{:S(2)}, u32[]{:S(2)}) %collective-permute-start.7) | collective-permute-done | bytes 262176 | tf_op jit(solution)/shard_map/cond/branch_3_fun/ppermute | solution.py:510
  35.9 2.2 %branch_3_fun.15 = (f32[2,2,2,448,128]{4,3,2,1,0:T(8,128)S(1)}, f32[2,2,2,448,128]{4,3,2,1,0:T(8,128)S(1)}) custom-call(s32[11]{0:T(128)S(4)} %get-tuple-element.145.refs_0_.info, bf16[8192,128]{1,0:T(8,128)(2,1)} %get-tuple-element.146.refs_1_.stored, ...), custom_call_target="tpu_custom_call", output_to_operand_aliasing={{0}: (9, {}), {1}: (10, {})} | custom-call | tf_op jit(solution)/shard_map/cond/branch_3_fun/pallas_call | solution.py:486
  38.0 3.4 %collective-permute-done.6.refs_7_ = bf16[256,512]{1,0:T(8,128)(2,1)S(1)} collective-permute-done((bf16[256,512]{1,0:T(8,128)(2,1)S(1)}, bf16[256,512]{1,0:T(8,128)(2,1)S(1)}, u32[]{:S(2)}, u32[]{:S(2)}) %collective-permute-start.6) | collective-permute-done | bytes 262176 | tf_op jit(solution)/shard_map/cond/branch_3_fun/ppermute | solution.py:510
  41.5 2.2 %branch_3_fun.16 = (f32[2,2,2,448,128]{4,3,2,1,0:T(8,128)S(1)}, f32[2,2,2,448,128]{4,3,2,1,0:T(8,128)S(1)}) custom-call(s32[11]{0:T(128)S(4)} %get-tuple-element.145.refs_0_.info, bf16[8192,128]{1,0:T(8,128)(2,1)} %get-tuple-element.146.refs_1_.stored, ...), custom_call_target="tpu_custom_call", output_to_operand_aliasing={{0}: (9, {}), {1}: (10, {})} | custom-call | tf_op jit(solution)/shard_map/cond/branch_3_fun/pallas_call | solution.py:486
  43.6 0.2 branch_3_fun.17
  44.1 0.9 %collective-permute-start.14 = (bf16[2,2,448,128]{3,2,1,0:T(8,128)(2,1)S(1)}, bf16[2,2,448,128]{3,2,1,0:T(8,128)(2,1)S(1)}, u32[]{:S(2)}, u32[]{:S(2)}) collective-permute-start(bf16[2,2,448,128]{3,2,1,0:T(8,128)(2,1)S(1)} %get-tuple-element.199), channel_id=1, source_target_pairs={{0,1},{1,0},{2,3},{3,2},{4,5},{5,4},{6,7},{7,6},{8,9},{9,8},{10,11... | collective-permute-start | bytes 1376264 | tf_op jit(solution)/shard_map/ppermute | solution.py:507
  45.0 0.0 collective-permute-start.13
  45.0 1.4 %collective-permute-done.14.rim = bf16[2,2,448,128]{3,2,1,0:T(8,128)(2,1)S(1)} collective-permute-done((bf16[2,2,448,128]{3,2,1,0:T(8,128)(2,1)S(1)}, bf16[2,2,448,128]{3,2,1,0:T(8,128)(2,1)S(1)}, u32[]{:S(2)}, u32[]{:S(2)}) %collective-permute-start.14) | collective-permute-done | bytes 458784 | tf_op jit(solution)/shard_map/ppermute | solution.py:507
  46.4 0.1 shard_map.66.mix_in
  46.5 11.3 %collective-permute-done.13.rim = bf16[2,2,448,128]{3,2,1,0:T(8,128)(2,1)S(1)} collective-permute-done((bf16[2,2,448,128]{3,2,1,0:T(8,128)(2,1)S(1)}, bf16[2,2,448,128]{3,2,1,0:T(8,128)(2,1)S(1)}, u32[]{:S(2)}, u32[]{:S(2)}) %collective-permute-start.13) | collective-permute-done | bytes 458784 | tf_op jit(solution)/shard_map/ppermute | solution.py:507
  57.8 1.1 %close.1 = (bf16[3584,128]{1,0:T(8,128)(2,1)}, f32[3584,128]{1,0:T(8,128)S(1)}) custom-call(s32[11]{0:T(128)S(4)} %get-tuple-element.190.info.refs_0_, bf16[2,2,2,448,128]{4,3,2,1,0:T(8,128)(2,1)S(1)} %get-tuple-element.197.own, bf16[2,2,448,128]{3,2,1,0:T(8,128)(2,1)S(1)} %collective-permute-done.13.rim, ...), custom_call_target="tpu_custom_call", output_to_operand_aliasing={{1}: (3, {})} | custom-call | tf_op jit(solution)/shard_map/close/pallas_call | solution.py:632
Async XLA Ops:
  0.0 13.0 %copy-start = (bf16[4,128,2,256]{3,2,1,0:T(2,128)(2,1)S(1)}, bf16[4,128,2,256]{3,2,1,0:T(2,128)(2,1)}, u32[]{:S(2)}) copy-start(bf16[4,128,2,256]{3,2,1,0:T(2,128)(2,1)} %param.10) | copy-start | bytes 1572868
  0.0 13.0 %collective-permute-start.12 = (bf16[4,128,2,256]{3,2,1,0:T(2,128)(2,1)}, bf16[4,128,2,256]{3,2,1,0:T(2,128)(2,1)S(1)}, u32[]{:S(2)}, u32[]{:S(2)}) collective-permute-start(bf16[4,128,2,256]{3,2,1,0:T(2,128)(2,1)} %param.10), channel_id=1, source_target_pairs={{0,16},{16,0},{1,17},{17,1},{2,18},{18,2},{3,19},{19,3},{4,20},{20... | collective-permute-start | bytes 1572872 | tf_op jit(solution)/shard_map/ppermute | solution.py:510
  1.8 13.2 %collective-permute-start.10 = (bf16[2,2,448,128]{3,2,1,0:T(8,128)(2,1)S(1)}, bf16[2,2,448,128]{3,2,1,0:T(8,128)(2,1)S(1)}, u32[]{:S(2)}, u32[]{:S(2)}) collective-permute-start(bf16[2,2,448,128]{3,2,1,0:T(8,128)(2,1)S(1)} %get-tuple-element.192), channel_id=1, source_target_pairs={{0,15},{1,2},{2,1},{3,4},{4,3},{5,6},{6,5},{7,8},{8,7},{9,10},{10,... | collective-permute-start | bytes 1376264 | tf_op jit(solution)/shard_map/ppermute | solution.py:507
  4.0 11.1 %collective-permute-start.11 = (bf16[2,2,448,128]{3,2,1,0:T(8,128)(2,1)S(1)}, bf16[2,2,448,128]{3,2,1,0:T(8,128)(2,1)S(1)}, u32[]{:S(2)}, u32[]{:S(2)}) collective-permute-start(bf16[2,2,448,128]{3,2,1,0:T(8,128)(2,1)S(1)} %get-tuple-element.193), channel_id=1, source_target_pairs={{0,1},{1,0},{2,3},{3,2},{4,5},{5,4},{6,7},{7,6},{8,9},{9,8},{10,11... | collective-permute-start | bytes 1376264 | tf_op jit(solution)/shard_map/ppermute | solution.py:507
  16.1 9.8 %collective-permute-start.9 = (bf16[256,512]{1,0:T(8,128)(2,1)S(1)}, bf16[256,512]{1,0:T(8,128)(2,1)S(1)}, u32[]{:S(2)}, u32[]{:S(2)}) collective-permute-start(bf16[256,512]{1,0:T(8,128)(2,1)S(1)} %get-tuple-element.169), channel_id=1, source_target_pairs={{16,0},{0,16},{17,1},{1,17},{18,2},{2,18},{19,3},{3,19},{20,4},{4,... | collective-permute-start | bytes 786440 | tf_op jit(solution)/shard_map/cond/branch_3_fun/ppermute | solution.py:510
  20.2 10.0 %collective-permute-start.8 = (bf16[256,512]{1,0:T(8,128)(2,1)S(1)}, bf16[256,512]{1,0:T(8,128)(2,1)S(1)}, u32[]{:S(2)}, u32[]{:S(2)}) collective-permute-start(bf16[256,512]{1,0:T(8,128)(2,1)S(1)} %get-tuple-element.164), channel_id=1, source_target_pairs={{16,0},{0,16},{17,1},{1,17},{18,2},{2,18},{19,3},{3,19},{20,4},{4,... | collective-permute-start | bytes 786440 | tf_op jit(solution)/shard_map/cond/branch_3_fun/ppermute | solution.py:510
  22.3 13.6 %collective-permute-start.7 = (bf16[256,512]{1,0:T(8,128)(2,1)S(1)}, bf16[256,512]{1,0:T(8,128)(2,1)S(1)}, u32[]{:S(2)}, u32[]{:S(2)}) collective-permute-start(bf16[256,512]{1,0:T(8,128)(2,1)S(1)} %get-tuple-element.160), channel_id=1, source_target_pairs={{16,0},{0,16},{17,1},{1,17},{18,2},{2,18},{19,3},{3,19},{20,4},{4,... | collective-permute-start | bytes 786440 | tf_op jit(solution)/shard_map/cond/branch_3_fun/ppermute | solution.py:510
  25.8 15.7 %collective-permute-start.6 = (bf16[256,512]{1,0:T(8,128)(2,1)S(1)}, bf16[256,512]{1,0:T(8,128)(2,1)S(1)}, u32[]{:S(2)}, u32[]{:S(2)}) collective-permute-start(bf16[256,512]{1,0:T(8,128)(2,1)S(1)} %get-tuple-element.156), channel_id=1, source_target_pairs={{16,0},{0,16},{17,1},{1,17},{18,2},{2,18},{19,3},{3,19},{20,4},{4,... | collective-permute-start | bytes 786440 | tf_op jit(solution)/shard_map/cond/branch_3_fun/ppermute | solution.py:510
  44.1 2.3 %collective-permute-start.14 = (bf16[2,2,448,128]{3,2,1,0:T(8,128)(2,1)S(1)}, bf16[2,2,448,128]{3,2,1,0:T(8,128)(2,1)S(1)}, u32[]{:S(2)}, u32[]{:S(2)}) collective-permute-start(bf16[2,2,448,128]{3,2,1,0:T(8,128)(2,1)S(1)} %get-tuple-element.199), channel_id=1, source_target_pairs={{0,1},{1,0},{2,3},{3,2},{4,5},{5,4},{6,7},{7,6},{8,9},{9,8},{10,11... | collective-permute-start | bytes 1376264 | tf_op jit(solution)/shard_map/ppermute | solution.py:507
  45.0 12.8 %collective-permute-start.13 = (bf16[2,2,448,128]{3,2,1,0:T(8,128)(2,1)S(1)}, bf16[2,2,448,128]{3,2,1,0:T(8,128)(2,1)S(1)}, u32[]{:S(2)}, u32[]{:S(2)}) collective-permute-start(bf16[2,2,448,128]{3,2,1,0:T(8,128)(2,1)S(1)} %get-tuple-element.198), channel_id=1, source_target_pairs={{0,15},{1,2},{2,1},{3,4},{4,3},{5,6},{6,5},{7,8},{8,7},{9,10},{10,... | collective-permute-start | bytes 1376264 | tf_op jit(solution)/shard_map/ppermute | solution.py:507
where the time goes:
time: 59.2 us; the launch traced here: 59.1 us
  waiting for transfers between devices  29 us (49%)
  Pallas kernels  21.4 us (36%)
  starting transfers between devices  6.93 us (12%)
  between operations  0.87 us (1%)
  local copies, waits for them, and re-layouts  0.61 us (1%)
    pallas_call x12, Pallas kernels, kernel_call(): pl.pallas_call(body, out_shape=out, in_specs=[SMEM] * len(scalars) + [HBM...  18.7 us
    ppermute x5, waiting for transfers between devices, swap(): return lax.ppermute(x, 'depth', [(one, other), (other, one)])  15.2 us
    ppermute x4, waiting for transfers between devices, moved(): return lax.ppermute(x, 'tile', pairs)  13.8 us
    ppermute x5, starting transfers between devices, swap(): return lax.ppermute(x, 'depth', [(one, other), (other, one)])  3.87 us
    ppermute x4, starting transfers between devices, moved(): return lax.ppermute(x, 'tile', pairs)  3.06 us
    pallas_call x1, Pallas kernels, on_device(): pl.pallas_call(first_kernel, out_shape=(*edge_shapes, pltpu.SMEM((3 + 2 *...  1.58 us
  transfers between devices with their start and end apart: 9, of which 7 were waited for; matrix products, arithmetic and copies ran while one was open for 1% of the time, Pallas kernels for 29%

commit v1 on v0

--- a/solution.py
+++ b/solution.py
@@ -10,6 +10,7 @@
 
 LANES = 128
 CHUNK = 64
+WIDE_CHUNK = 256
 STEP = 32
 PACKED = 16
 F32 = jnp.float32
@@ -210,14 +211,14 @@
         side += count
 
     def move(i, carry):
-        a = pl.multiple_of(i * CHUNK, CHUNK)
+        a = pl.multiple_of(i * WIDE_CHUNK, WIDE_CHUNK)
         for c in range(2):
-            halves = [wide[pl.ds(a * 4 + ct * 2 + c, CHUNK, stride=4), :] for ct in range(2)]
+            halves = [wide[pl.ds(a * 4 + ct * 2 + c, WIDE_CHUNK, stride=4), :] for ct in range(2)]
             value = pltpu.roll(jnp.concatenate(halves, axis=1), place.col, 1)
-            write(c, pl.ds(a, CHUNK), value.astype(BF16))
+            write(c, pl.ds(a, WIDE_CHUNK), value.astype(BF16))
         return carry
 
-    lax.fori_loop(0, side // CHUNK, move, 0)
+    lax.fori_loop(0, side // WIDE_CHUNK, move, 0)
 
 
 def unpack_stored(place, j, cap, stored, planes, packed, sems, wide):

time: 59.2 us -> 58.3 us (0.985)
  Pallas kernels: 21.4 us -> 18.5 us
  waiting for transfers between devices: 29 us -> 31.5 us
    pallas_call x12, Pallas kernels: 18.7 us -> 15.8 us  [kernel_call(): pl.pallas_call(body, out_shape=out, in_specs=[SMEM] * len(scalars) + [HBM...]
    ppermute x5, waiting for transfers between devices: 15.2 us -> 17.4 us  [swap(): return lax.ppermute(x, 'depth', [(one, other), (other, one)])]
    ppermute x5, starting transfers between devices: 3.87 us -> 3.18 us  [swap(): return lax.ppermute(x, 'depth', [(one, other), (other, one)])]
  transfers between devices with their start and end apart: 9 -> 9, of which waited for: 7 -> 7; matrix products, arithmetic and copies ran while one was open for 1% -> 1% of each run, Pallas kernels for 29% -> 25%
where the time goes in v1:
time: 58.3 us; the launch traced here: 58.2 us
  waiting for transfers between devices  31.5 us (54%)
  Pallas kernels  18.5 us (32%)
  starting transfers between devices  6.36 us (11%)
  between operations  0.87 us (1%)
  local copies, waits for them, and re-layouts  0.61 us (1%)
    ppermute x5, waiting for transfers between devices, swap(): return lax.ppermute(x, 'depth', [(one, other), (other, one)])  17.4 us
    pallas_call x12, Pallas kernels, kernel_call(): pl.pallas_call(body, out_shape=out, in_specs=[SMEM] * len(scalars) + [HBM...  15.8 us
    ppermute x4, waiting for transfers between devices, moved(): return lax.ppermute(x, 'tile', pairs)  14.1 us
    ppermute x5, starting transfers between devices, swap(): return lax.ppermute(x, 'depth', [(one, other), (other, one)])  3.18 us
    ppermute x4, starting transfers between devices, moved(): return lax.ppermute(x, 'tile', pairs)  3.18 us
    pallas_call x1, Pallas kernels, on_device(): pl.pallas_call(first_kernel, out_shape=(*edge_shapes, pltpu.SMEM((3 + 2 *...  1.58 us
  transfers between devices with their start and end apart: 9, of which 7 were waited for; matrix products, arithmetic and copies ran while one was open for 1% of the time, Pallas kernels for 25%

profile of v1, /device:TPU:19, one launch (start us, length us, event | category | flops | bytes accessed | tf_op | source)
XLA Modules:
  0.0 58.2 jit_solution(3808214694666680482)
XLA Ops:
  0.0 0.0 copy-start
  0.0 0.3 collective-permute-start.12
  0.3 1.6 %first.1 = (bf16[2,2,448,128]{3,2,1,0:T(8,128)(2,1)S(1)}, bf16[2,2,448,128]{3,2,1,0:T(8,128)(2,1)S(1)}, s32[11]{0:T(128)S(4)}, f32[2,2,31]{2,1,0:T(2,128)S(4)}, f32[3584,128]{1,0:T(8,128)S(1)}) custom-call(s32[16]{0:T(128)} %counts.1, s32[2,64]{1,0:T(2,128)} %bitcast.40, f32[2,2,31]{2,1,0:T(2,128)} %taps.1, f32[3584,128]{1,0:T(8,128)} %bitcast.39), custom_call_target="tpu_custom_call" | custom-call | tf_op jit(solution)/shard_map/first/pallas_call | solution.py:522
  1.8 2.1 %collective-permute-start.10 = (bf16[2,2,448,128]{3,2,1,0:T(8,128)(2,1)S(1)}, bf16[2,2,448,128]{3,2,1,0:T(8,128)(2,1)S(1)}, u32[]{:S(2)}, u32[]{:S(2)}) collective-permute-start(bf16[2,2,448,128]{3,2,1,0:T(8,128)(2,1)S(1)} %get-tuple-element.192), channel_id=1, source_target_pairs={{0,15},{1,2},{2,1},{3,4},{4,3},{5,6},{6,5},{7,8},{8,7},{9,10},{10,... | collective-permute-start | bytes 1376264 | tf_op jit(solution)/shard_map/ppermute | solution.py:508
  4.0 0.0 collective-permute-start.11
  4.0 0.6 %slice.3 = s32[1]{0:T(128)} slice(s32[11]{0:T(128)S(4)} %get-tuple-element.190.info.refs_0_), slice={[2:3]} | slice | bytes 8 | tf_op jit(solution)/shard_map/slice | solution.py:628
  4.6 1.4 %shard_map.64 = (bf16[4,512,512]{2,1,0:T(8,128)(2,1)S(1)}, bf16[256,512]{1,0:T(8,128)(2,1)S(1)}) custom-call(s32[11]{0:T(128)S(4)} %get-tuple-element.190.info.refs_0_, f32[2,2,31]{2,1,0:T(2,128)S(4)} %get-tuple-element.194.taps), custom_call_target="tpu_custom_call" | custom-call | tf_op jit(solution)/shard_map/pallas_call | solution.py:487
  6.6 6.4 %collective-permute-done.12 = bf16[4,128,2,256]{3,2,1,0:T(2,128)(2,1)S(1)} collective-permute-done((bf16[4,128,2,256]{3,2,1,0:T(2,128)(2,1)}, bf16[4,128,2,256]{3,2,1,0:T(2,128)(2,1)S(1)}, u32[]{:S(2)}, u32[]{:S(2)}) %collective-permute-start.12) | collective-permute-done | bytes 524320 | tf_op jit(solution)/shard_map/ppermute | solution.py:511
  13.0 0.0 copy-done
  13.0 0.6 %shard_map.65 = f32[1,256,512]{2,1,0:T(8,128)S(1)} custom-call(s32[11]{0:T(128)S(4)} %get-tuple-element.190.info.refs_0_, bf16[4,512,512]{2,1,0:T(8,128)(2,1)S(1)} %get-tuple-element.195.refs_1_, bf16[256,512]{1,0:T(8,128)(2,1)S(1)} %get-tuple-element.196.refs_2_, bf16[2048,128]{1,0:T(8,128)(2,1)S(1)} %bitcast.31, bf16[2048,128]{1,0:T(8,128)(2,1)S(1)} %bitcast.27), custom_call_target="tpu_custom_call" | custom-call | tf_op jit(solution)/shard_map/pallas_call | solution.py:487
  13.7 1.4 %collective-permute-done.10 = bf16[2,2,448,128]{3,2,1,0:T(8,128)(2,1)S(1)} collective-permute-done((bf16[2,2,448,128]{3,2,1,0:T(8,128)(2,1)S(1)}, bf16[2,2,448,128]{3,2,1,0:T(8,128)(2,1)S(1)}, u32[]{:S(2)}, u32[]{:S(2)}) %collective-permute-start.10) | collective-permute-done | bytes 458784 | tf_op jit(solution)/shard_map/ppermute | solution.py:508
  15.1 0.0 collective-permute-done.11
  15.1 27.9 %conditional.1 = ((bf16[2,2,448,128]{3,2,1,0:T(8,128)(2,1)S(1)}, bf16[2,2,448,128]{3,2,1,0:T(8,128)(2,1)S(1)}, bf16[2,2,2,448,128]{4,3,2,1,0:T(8,128)(2,1)S(1)})) conditional(s32[]{:T(128)} %bitcast.4, (s32[11]{0:T(128)S(4)}, bf16[8192,128]{1,0:T(8,128)(2,1)}, f32[3584,128]{1,0:T(8,128)S(1)}, ...), branch_computations={%region_0.0_spmd, %region_1.0_spmd, %region_2.0_spmd, %region_3.0_... | conditional | bytes 4194472 | solution.py:628
  15.1 1.0 %branch_3_fun.12 = (bf16[256,512]{1,0:T(8,128)(2,1)S(1)}, f32[2,256,512]{2,1,0:T(8,128)S(1)}, bf16[2,2,256,256]{3,2,1,0:T(8,128)(2,1)S(1)}, f32[2,2,272,128]{3,2,1,0:T(8,128)S(1)}) custom-call(s32[11]{0:T(128)S(4)} %get-tuple-element.145.refs_0_.info, bf16[8192,128]{1,0:T(8,128)(2,1)} %get-tuple-element.146.refs_1_.stored, ...), custom_call_target="tpu_custom_call" | custom-call | tf_op jit(solution)/shard_map/cond/branch_3_fun/pallas_call | solution.py:487
  16.1 1.6 %collective-permute-start.9 = (bf16[256,512]{1,0:T(8,128)(2,1)S(1)}, bf16[256,512]{1,0:T(8,128)(2,1)S(1)}, u32[]{:S(2)}, u32[]{:S(2)}) collective-permute-start(bf16[256,512]{1,0:T(8,128)(2,1)S(1)} %get-tuple-element.169), channel_id=1, source_target_pairs={{16,0},{0,16},{17,1},{1,17},{18,2},{2,18},{19,3},{3,19},{20,4},{4,... | collective-permute-start | bytes 786440 | tf_op jit(solution)/shard_map/cond/branch_3_fun/ppermute | solution.py:511
  17.7 1.9 %branch_3_fun.11 = (bf16[256,512]{1,0:T(8,128)(2,1)S(1)}, f32[2,256,512]{2,1,0:T(8,128)S(1)}, bf16[2,2,256,256]{3,2,1,0:T(8,128)(2,1)S(1)}, f32[2,2,272,128]{3,2,1,0:T(8,128)S(1)}) custom-call(s32[11]{0:T(128)S(4)} %get-tuple-element.145.refs_0_.info, bf16[8192,128]{1,0:T(8,128)(2,1)} %get-tuple-element.146.refs_1_.stored, ...), custom_call_target="tpu_custom_call" | custom-call | tf_op jit(solution)/shard_map/cond/branch_3_fun/pallas_call | solution.py:487
  19.7 0.1 collective-permute-start.8
  19.8 1.8 %branch_3_fun.10 = (bf16[256,512]{1,0:T(8,128)(2,1)S(1)}, f32[2,256,512]{2,1,0:T(8,128)S(1)}, bf16[2,2,256,256]{3,2,1,0:T(8,128)(2,1)S(1)}, f32[2,2,272,128]{3,2,1,0:T(8,128)S(1)}) custom-call(s32[11]{0:T(128)S(4)} %get-tuple-element.145.refs_0_.info, bf16[8192,128]{1,0:T(8,128)(2,1)} %get-tuple-element.146.refs_1_.stored, ...), custom_call_target="tpu_custom_call" | custom-call | tf_op jit(solution)/shard_map/cond/branch_3_fun/pallas_call | solution.py:487
  21.6 1.1 %collective-permute-start.7 = (bf16[256,512]{1,0:T(8,128)(2,1)S(1)}, bf16[256,512]{1,0:T(8,128)(2,1)S(1)}, u32[]{:S(2)}, u32[]{:S(2)}) collective-permute-start(bf16[256,512]{1,0:T(8,128)(2,1)S(1)} %get-tuple-element.160), channel_id=1, source_target_pairs={{16,0},{0,16},{17,1},{1,17},{18,2},{2,18},{19,3},{3,19},{20,4},{4,... | collective-permute-start | bytes 786440 | tf_op jit(solution)/shard_map/cond/branch_3_fun/ppermute | solution.py:511
  22.7 1.7 %branch_3_fun.9 = (bf16[256,512]{1,0:T(8,128)(2,1)S(1)}, f32[2,256,512]{2,1,0:T(8,128)S(1)}, bf16[2,2,256,256]{3,2,1,0:T(8,128)(2,1)S(1)}, f32[2,2,272,128]{3,2,1,0:T(8,128)S(1)}) custom-call(s32[11]{0:T(128)S(4)} %get-tuple-element.145.refs_0_.info, bf16[8192,128]{1,0:T(8,128)(2,1)} %get-tuple-element.146.refs_1_.stored, ...), custom_call_target="tpu_custom_call" | custom-call | tf_op jit(solution)/shard_map/cond/branch_3_fun/pallas_call | solution.py:487
  24.4 0.1 collective-permute-start.6
  24.5 0.0 collective-permute-done.9.refs_7_
  24.6 1.9 %branch_3_fun.13 = (f32[2,2,2,448,128]{4,3,2,1,0:T(8,128)S(1)}, f32[2,2,2,448,128]{4,3,2,1,0:T(8,128)S(1)}) custom-call(s32[11]{0:T(128)S(4)} %get-tuple-element.145.refs_0_.info, bf16[8192,128]{1,0:T(8,128)(2,1)} %get-tuple-element.146.refs_1_.stored, f32[3584,128]{1,0:T(8,128)S(1)} %get-tuple-element.147.refs_2_.obj, ...), custom_call_target="tpu_custom_call" | custom-call | tf_op jit(solution)/shard_map/cond/branch_3_fun/pallas_call | solution.py:487
  26.5 3.2 %collective-permute-done.8.refs_7_ = bf16[256,512]{1,0:T(8,128)(2,1)S(1)} collective-permute-done((bf16[256,512]{1,0:T(8,128)(2,1)S(1)}, bf16[256,512]{1,0:T(8,128)(2,1)S(1)}, u32[]{:S(2)}, u32[]{:S(2)}) %collective-permute-start.8) | collective-permute-done | bytes 262176 | tf_op jit(solution)/shard_map/cond/branch_3_fun/ppermute | solution.py:511
  29.7 1.7 %branch_3_fun.14 = (f32[2,2,2,448,128]{4,3,2,1,0:T(8,128)S(1)}, f32[2,2,2,448,128]{4,3,2,1,0:T(8,128)S(1)}) custom-call(s32[11]{0:T(128)S(4)} %get-tuple-element.145.refs_0_.info, bf16[8192,128]{1,0:T(8,128)(2,1)} %get-tuple-element.146.refs_1_.stored, ...), custom_call_target="tpu_custom_call", output_to_operand_aliasing={{0}: (9, {}), {1}: (10, {})} | custom-call | tf_op jit(solution)/shard_map/cond/branch_3_fun/pallas_call | solution.py:487
  31.4 3.9 %collective-permute-done.7.refs_7_ = bf16[256,512]{1,0:T(8,128)(2,1)S(1)} collective-permute-done((bf16[256,512]{1,0:T(8,128)(2,1)S(1)}, bf16[256,512]{1,0:T(8,128)(2,1)S(1)}, u32[]{:S(2)}, u32[]{:S(2)}) %collective-permute-start.7) | collective-permute-done | bytes 262176 | tf_op jit(solution)/shard_map/cond/branch_3_fun/ppermute | solution.py:511
  35.3 1.7 %branch_3_fun.15 = (f32[2,2,2,448,128]{4,3,2,1,0:T(8,128)S(1)}, f32[2,2,2,448,128]{4,3,2,1,0:T(8,128)S(1)}) custom-call(s32[11]{0:T(128)S(4)} %get-tuple-element.145.refs_0_.info, bf16[8192,128]{1,0:T(8,128)(2,1)} %get-tuple-element.146.refs_1_.stored, ...), custom_call_target="tpu_custom_call", output_to_operand_aliasing={{0}: (9, {}), {1}: (10, {})} | custom-call | tf_op jit(solution)/shard_map/cond/branch_3_fun/pallas_call | solution.py:487
  37.0 3.9 %collective-permute-done.6.refs_7_ = bf16[256,512]{1,0:T(8,128)(2,1)S(1)} collective-permute-done((bf16[256,512]{1,0:T(8,128)(2,1)S(1)}, bf16[256,512]{1,0:T(8,128)(2,1)S(1)}, u32[]{:S(2)}, u32[]{:S(2)}) %collective-permute-start.6) | collective-permute-done | bytes 262176 | tf_op jit(solution)/shard_map/cond/branch_3_fun/ppermute | solution.py:511
  40.9 1.7 %branch_3_fun.16 = (f32[2,2,2,448,128]{4,3,2,1,0:T(8,128)S(1)}, f32[2,2,2,448,128]{4,3,2,1,0:T(8,128)S(1)}) custom-call(s32[11]{0:T(128)S(4)} %get-tuple-element.145.refs_0_.info, bf16[8192,128]{1,0:T(8,128)(2,1)} %get-tuple-element.146.refs_1_.stored, ...), custom_call_target="tpu_custom_call", output_to_operand_aliasing={{0}: (9, {}), {1}: (10, {})} | custom-call | tf_op jit(solution)/shard_map/cond/branch_3_fun/pallas_call | solution.py:487
  42.6 0.2 branch_3_fun.17
  43.0 1.0 %collective-permute-start.14 = (bf16[2,2,448,128]{3,2,1,0:T(8,128)(2,1)S(1)}, bf16[2,2,448,128]{3,2,1,0:T(8,128)(2,1)S(1)}, u32[]{:S(2)}, u32[]{:S(2)}) collective-permute-start(bf16[2,2,448,128]{3,2,1,0:T(8,128)(2,1)S(1)} %get-tuple-element.199), channel_id=1, source_target_pairs={{0,1},{1,0},{2,3},{3,2},{4,5},{5,4},{6,7},{7,6},{8,9},{9,8},{10,11... | collective-permute-start | bytes 1376264 | tf_op jit(solution)/shard_map/ppermute | solution.py:508
  44.0 0.0 collective-permute-start.13
  44.0 1.4 %collective-permute-done.14.rim = bf16[2,2,448,128]{3,2,1,0:T(8,128)(2,1)S(1)} collective-permute-done((bf16[2,2,448,128]{3,2,1,0:T(8,128)(2,1)S(1)}, bf16[2,2,448,128]{3,2,1,0:T(8,128)(2,1)S(1)}, u32[]{:S(2)}, u32[]{:S(2)}) %collective-permute-start.14) | collective-permute-done | bytes 458784 | tf_op jit(solution)/shard_map/ppermute | solution.py:508
  45.5 0.1 shard_map.66.mix_in
  45.6 11.3 %collective-permute-done.13.rim = bf16[2,2,448,128]{3,2,1,0:T(8,128)(2,1)S(1)} collective-permute-done((bf16[2,2,448,128]{3,2,1,0:T(8,128)(2,1)S(1)}, bf16[2,2,448,128]{3,2,1,0:T(8,128)(2,1)S(1)}, u32[]{:S(2)}, u32[]{:S(2)}) %collective-permute-start.13) | collective-permute-done | bytes 458784 | tf_op jit(solution)/shard_map/ppermute | solution.py:508
  56.9 1.1 %close.1 = (bf16[3584,128]{1,0:T(8,128)(2,1)}, f32[3584,128]{1,0:T(8,128)S(1)}) custom-call(s32[11]{0:T(128)S(4)} %get-tuple-element.190.info.refs_0_, bf16[2,2,2,448,128]{4,3,2,1,0:T(8,128)(2,1)S(1)} %get-tuple-element.197.own, bf16[2,2,448,128]{3,2,1,0:T(8,128)(2,1)S(1)} %collective-permute-done.13.rim, ...), custom_call_target="tpu_custom_call", output_to_operand_aliasing={{1}: (3, {})} | custom-call | tf_op jit(solution)/shard_map/close/pallas_call | solution.py:633
Async XLA Ops:
  0.0 13.0 %copy-start = (bf16[4,128,2,256]{3,2,1,0:T(2,128)(2,1)S(1)}, bf16[4,128,2,256]{3,2,1,0:T(2,128)(2,1)}, u32[]{:S(2)}) copy-start(bf16[4,128,2,256]{3,2,1,0:T(2,128)(2,1)} %param.10) | copy-start | bytes 1572868
  0.0 13.0 %collective-permute-start.12 = (bf16[4,128,2,256]{3,2,1,0:T(2,128)(2,1)}, bf16[4,128,2,256]{3,2,1,0:T(2,128)(2,1)S(1)}, u32[]{:S(2)}, u32[]{:S(2)}) collective-permute-start(bf16[4,128,2,256]{3,2,1,0:T(2,128)(2,1)} %param.10), channel_id=1, source_target_pairs={{0,16},{16,0},{1,17},{17,1},{2,18},{18,2},{3,19},{19,3},{4,20},{20... | collective-permute-start | bytes 1572872 | tf_op jit(solution)/shard_map/ppermute | solution.py:511
  1.8 13.2 %collective-permute-start.10 = (bf16[2,2,448,128]{3,2,1,0:T(8,128)(2,1)S(1)}, bf16[2,2,448,128]{3,2,1,0:T(8,128)(2,1)S(1)}, u32[]{:S(2)}, u32[]{:S(2)}) collective-permute-start(bf16[2,2,448,128]{3,2,1,0:T(8,128)(2,1)S(1)} %get-tuple-element.192), channel_id=1, source_target_pairs={{0,15},{1,2},{2,1},{3,4},{4,3},{5,6},{6,5},{7,8},{8,7},{9,10},{10,... | collective-permute-start | bytes 1376264 | tf_op jit(solution)/shard_map/ppermute | solution.py:508
  4.0 11.1 %collective-permute-start.11 = (bf16[2,2,448,128]{3,2,1,0:T(8,128)(2,1)S(1)}, bf16[2,2,448,128]{3,2,1,0:T(8,128)(2,1)S(1)}, u32[]{:S(2)}, u32[]{:S(2)}) collective-permute-start(bf16[2,2,448,128]{3,2,1,0:T(8,128)(2,1)S(1)} %get-tuple-element.193), channel_id=1, source_target_pairs={{0,1},{1,0},{2,3},{3,2},{4,5},{5,4},{6,7},{7,6},{8,9},{9,8},{10,11... | collective-permute-start | bytes 1376264 | tf_op jit(solution)/shard_map/ppermute | solution.py:508
  16.1 8.4 %collective-permute-start.9 = (bf16[256,512]{1,0:T(8,128)(2,1)S(1)}, bf16[256,512]{1,0:T(8,128)(2,1)S(1)}, u32[]{:S(2)}, u32[]{:S(2)}) collective-permute-start(bf16[256,512]{1,0:T(8,128)(2,1)S(1)} %get-tuple-element.169), channel_id=1, source_target_pairs={{16,0},{0,16},{17,1},{1,17},{18,2},{2,18},{19,3},{3,19},{20,4},{4,... | collective-permute-start | bytes 786440 | tf_op jit(solution)/shard_map/cond/branch_3_fun/ppermute | solution.py:511
  19.7 10.0 %collective-permute-start.8 = (bf16[256,512]{1,0:T(8,128)(2,1)S(1)}, bf16[256,512]{1,0:T(8,128)(2,1)S(1)}, u32[]{:S(2)}, u32[]{:S(2)}) collective-permute-start(bf16[256,512]{1,0:T(8,128)(2,1)S(1)} %get-tuple-element.164), channel_id=1, source_target_pairs={{16,0},{0,16},{17,1},{1,17},{18,2},{2,18},{19,3},{3,19},{20,4},{4,... | collective-permute-start | bytes 786440 | tf_op jit(solution)/shard_map/cond/branch_3_fun/ppermute | solution.py:511
  21.6 13.7 %collective-permute-start.7 = (bf16[256,512]{1,0:T(8,128)(2,1)S(1)}, bf16[256,512]{1,0:T(8,128)(2,1)S(1)}, u32[]{:S(2)}, u32[]{:S(2)}) collective-permute-start(bf16[256,512]{1,0:T(8,128)(2,1)S(1)} %get-tuple-element.160), channel_id=1, source_target_pairs={{16,0},{0,16},{17,1},{1,17},{18,2},{2,18},{19,3},{3,19},{20,4},{4,... | collective-permute-start | bytes 786440 | tf_op jit(solution)/shard_map/cond/branch_3_fun/ppermute | solution.py:511
  24.4 16.5 %collective-permute-start.6 = (bf16[256,512]{1,0:T(8,128)(2,1)S(1)}, bf16[256,512]{1,0:T(8,128)(2,1)S(1)}, u32[]{:S(2)}, u32[]{:S(2)}) collective-permute-start(bf16[256,512]{1,0:T(8,128)(2,1)S(1)} %get-tuple-element.156), channel_id=1, source_target_pairs={{16,0},{0,16},{17,1},{1,17},{18,2},{2,18},{19,3},{3,19},{20,4},{4,... | collective-permute-start | bytes 786440 | tf_op jit(solution)/shard_map/cond/branch_3_fun/ppermute | solution.py:511
  43.0 2.5 %collective-permute-start.14 = (bf16[2,2,448,128]{3,2,1,0:T(8,128)(2,1)S(1)}, bf16[2,2,448,128]{3,2,1,0:T(8,128)(2,1)S(1)}, u32[]{:S(2)}, u32[]{:S(2)}) collective-permute-start(bf16[2,2,448,128]{3,2,1,0:T(8,128)(2,1)S(1)} %get-tuple-element.199), channel_id=1, source_target_pairs={{0,1},{1,0},{2,3},{3,2},{4,5},{5,4},{6,7},{7,6},{8,9},{9,8},{10,11... | collective-permute-start | bytes 1376264 | tf_op jit(solution)/shard_map/ppermute | solution.py:508
  44.0 12.8 %collective-permute-start.13 = (bf16[2,2,448,128]{3,2,1,0:T(8,128)(2,1)S(1)}, bf16[2,2,448,128]{3,2,1,0:T(8,128)(2,1)S(1)}, u32[]{:S(2)}, u32[]{:S(2)}) collective-permute-start(bf16[2,2,448,128]{3,2,1,0:T(8,128)(2,1)S(1)} %get-tuple-element.198), channel_id=1, source_target_pairs={{0,15},{1,2},{2,1},{3,4},{4,3},{5,6},{6,5},{7,8},{8,7},{9,10},{10,... | collective-permute-start | bytes 1376264 | tf_op jit(solution)/shard_map/ppermute | solution.py:508
